TPU v7x, 128 devices: a whole 4x4x4 slice. The times are simulated.
128 devices in a mesh: row: 8 (over z, x_hi), col: 16 (over x_lo, y, core).
Axes of the slice: x: 4 (x_hi: 2, x_lo: 2; x = x_hi * 2 + x_lo), y: 4, z: 4, core: 2. Of those that a mesh axis runs over, the one named last changes fastest.
Arguments:
- tile_blocks: bfloat16 [8, 16, 384, 128, 128], P('row', 'col'), may hold values from -0.109375 to 0.109375
- tile_rows: int32 [8, 16, 384], P('row', 'col'), may hold values from 0 to 127, as said below
- tile_cols: int32 [8, 16, 384], P('row', 'col'), may hold values from 0 to 63, as said below
- tile_count: int32 [8, 16], P('row', 'col'), may hold values from 48 to 384, as said below
- vectors: float32 [16, 131072], P(None, ('row', 'col')), may hold values from -8 to 8
- hvectors: float32 [16, 131072], P(None, ('row', 'col')), may hold values from -20 to 20
- previous: float32 [16, 131072], P(None, ('row', 'col')), may hold values from -6 to 6
- hprevious: float32 [16, 131072], P(None, ('row', 'col')), may hold values from -6 to 6
Outputs:
- orthonormal: float32 [48, 131072], P(None, ('row', 'col'))
- orthonormal_image: float32 [48, 131072], P(None, ('row', 'col'))
- projected: float32 [48, 48], replicated
Inputs may be any that keep to these rules, and one draw needn't show every extreme that they name: `tile_rows`: both ends occur in every draw. `tile_cols`: both ends occur in every draw. `tile_count`: one process cell holds exactly 384 live slots in every draw; every other cell holds between 48 and 192.
All inputs are finite; a program needn't handle non-finite values.
Results may differ from a plain program's by a relative error of at most 0.0003.
Values sent between devices are 32-bit elements; how exact they have to be, the bound alone decides.
No kernel may reach another device: no remote copies, remote signals or barrier semaphores. Data moves between devices by JAX's collectives and lax.ppermute only.
A program may use at most 64 MiB of HBM per device.

v0:
```python
import math
import jax
import jax.numpy as jnp
from jax import lax
from jax.sharding import PartitionSpec as P

EPSILON = 1e-06
HIGHEST_PRECISION = lax.Precision.HIGHEST


def dense_product(first, second):
    return jnp.dot(first, second, preferred_element_type=jnp.float32, precision=HIGHEST_PRECISION)


def hamiltonian(tile_blocks, tile_rows, tile_cols, tile_count, operand):
    tile_stack = tile_blocks[0, 0]
    row_ids = tile_rows[0, 0]
    col_ids = tile_cols[0, 0]
    slot_count = tile_stack.shape[0]
    tile_width = tile_stack.shape[-1]
    members = operand.shape[0]
    live_mask = lax.iota(jnp.int32, slot_count) < tile_count[0, 0]
    row_range = lax.all_gather(operand, "col", axis=1, tiled=True)
    col_range = lax.all_gather(operand, "row", axis=1, tiled=True)
    row_blocks = row_range.reshape(members, -1, tile_width)
    col_blocks = col_range.reshape(members, -1, tile_width)
    block_size = math.gcd(slot_count, 64)
    block_count = slot_count // block_size

    def slot_block(counter):
        start = counter * block_size
        tile_part = lax.dynamic_slice_in_dim(tile_stack, start, block_size, 0).astype(jnp.float32)
        row_part = lax.dynamic_slice_in_dim(row_ids, start, block_size, 0)
        col_part = lax.dynamic_slice_in_dim(col_ids, start, block_size, 0)
        live_part = lax.dynamic_slice_in_dim(live_mask, start, block_size, 0)[None, :, None]
        return (tile_part, row_part, col_part, live_part)

    def forward_product(tile_part, col_part):
        inputs = jnp.take(col_blocks, col_part, axis=1)
        return jnp.einsum("tij,mtj->mti", tile_part, inputs, precision=HIGHEST_PRECISION)

    def backward_product(tile_part, row_part):
        inputs = jnp.take(row_blocks, row_part, axis=1)
        return jnp.einsum("tij,mti->mtj", tile_part, inputs, precision=HIGHEST_PRECISION)

    def forward(counter, totals):
        tile_part, row_part, col_part, live_part = slot_block(counter)
        product = forward_product(tile_part, col_part)
        return totals.at[:, row_part, :].add(jnp.where(live_part, product, 0.0))

    def backward(counter, totals):
        tile_part, row_part, col_part, live_part = slot_block(counter)
        product = backward_product(tile_part, row_part)
        return totals.at[:, col_part, :].add(jnp.where(live_part, product, 0.0))

    zero_rows = jnp.zeros(row_blocks.shape, jnp.float32)
    zero_cols = jnp.zeros(col_blocks.shape, jnp.float32)
    row_totals = lax.fori_loop(0, block_count, forward, zero_rows)
    col_totals = lax.fori_loop(0, block_count, backward, zero_cols)
    applied = lax.psum_scatter(
        row_totals.reshape(members, -1), "col", scatter_dimension=1, tiled=True
    )
    applied = applied + lax.psum_scatter(
        col_totals.reshape(members, -1), "row", scatter_dimension=1, tiled=True
    )
    return applied


def on_device(
    tile_blocks, tile_rows, tile_cols, tile_count, vectors, hvectors, previous, hprevious
):
    total_rows = vectors.shape[1] * lax.axis_size("row") * lax.axis_size("col")
    rayleigh_top, rayleigh_bottom = lax.psum(
        (jnp.sum(vectors * hvectors, axis=1), jnp.sum(vectors * vectors, axis=1)), ("row", "col")
    )
    ritz_values = rayleigh_top / (rayleigh_bottom + EPSILON)
    residual = hvectors - ritz_values[:, None] * vectors
    residual_image = hamiltonian(tile_blocks, tile_rows, tile_cols, tile_count, residual)
    basis_rows = jnp.concatenate([vectors, residual, previous], axis=0)
    image_rows = jnp.concatenate([hvectors, residual_image, hprevious], axis=0)
    gram_matrix, mixed_matrix = lax.psum(
        (dense_product(basis_rows, basis_rows.T), dense_product(basis_rows, image_rows.T)),
        ("row", "col"),
    )
    factor = jnp.linalg.cholesky(gram_matrix)
    row_scale = math.sqrt(total_rows)
    orthonormal = row_scale * lax.linalg.triangular_solve(
        factor, basis_rows, left_side=True, lower=True
    )
    orthonormal_image = row_scale * lax.linalg.triangular_solve(
        factor, image_rows, left_side=True, lower=True
    )
    half_done = lax.linalg.triangular_solve(factor, mixed_matrix, left_side=True, lower=True)
    projected = lax.linalg.triangular_solve(
        factor, half_done, left_side=False, lower=True, transpose_a=True
    )
    return (orthonormal, orthonormal_image, projected)


def solution(mesh):
    in_specs = (
        P("row", "col", None, None, None),
        P("row", "col", None),
        P("row", "col", None),
        P("row", "col"),
        P(None, ("row", "col")),
        P(None, ("row", "col")),
        P(None, ("row", "col")),
        P(None, ("row", "col")),
    )
    out_specs = (P(None, ("row", "col")), P(None, ("row", "col")), P())
    return jax.shard_map(
        on_device, mesh=mesh, in_specs=in_specs, out_specs=out_specs, check_vma=False
    )
```

profile of v0, /device:TPU:1, one launch (start us, length us, event | category | flops | bytes accessed | tf_op | source)
XLA Modules:
  0.0 387.1 jit_solution(8466629798709150425)
XLA Ops:
  8.2 68.7 %all-reduce.1 = (f32[16]{0:T(128)S(1)}, f32[16]{0:T(128)S(1)}) all-reduce(f32[16]{0:T(128)S(1)} %get-tuple-element.269, f32[16]{0:T(128)S(1)} %get-tuple-element.268), channel_id=1, replica_groups=mesh['row'=8,'col'=16] {'row','col'}, use_global_device_ids=true, to_apply=%region_1.0 | all-reduce | flops 32 | bytes 256 | tf_op jit(solution)/shard_map/psum | solution.py:73
  78.5 31.3 %all_gather.6 = f32[16,8192]{1,0:T(8,128)S(1)} all-gather(f32[16,1024]{1,0:T(8,128)} %multiply_subtract_fusion), channel_id=1, replica_groups=mesh['row'=8,'col'=16] {'row'}, dimensions={1}, use_global_device_ids=true | all-gather | bytes 589824 | tf_op jit(solution)/shard_map/all_gather | solution.py:24
  112.0 52.6 %while.26 = (s32[]{:T(128)}, f32[16,128,128]{2,0,1:T(8,128)S(1)}, s32[384]{0:T(512)S(1)}, pred[384]{0:T(512)(128)(4,1)S(1)}, s32[384]{0:T(512)S(1)}, /*index=5*/...) while((s32[]{:T(128)}, f32[16,128,128]{2,0,1:T(8,128)S(1)}, ...), condition=%wide.region_9.11_spmd, body=%wide.region_7.10_spmd.sunk | while | flops 201721408 | bytes 5773547 | solution.py:58
  112.9 5.0 %fusion.50 = f32[64,16,128]{2,1,0:T(8,128)S(1)} fusion(bf16[384,128,128]{2,1,0:T(8,128)(2,1)} %get-tuple-element.428, s32[]{:T(128)S(6)} %select_n.125, f32[64,16,128]{2,1,0:T(8,128)S(1)} %gather_fusion, pred[64]{0:T(512)(128)(4,1)S(1)} %get-tuple-element.390, pred[64]{0:T(512)(128)(4,1)S(1)} %dynamic_slice.78), kind=kOutput, calls=%fused_computation.6.clone.1 | convolution fusion | flops 201588736 | bytes 3145860 | tf_op jit(solution)/shard_map/while/body/eval_jaxpr/tij,mtj->mti/dot_general | solution.py:40
  117.9 2.9 scatter_fusion
  121.6 5.0 %fusion.50 = f32[64,16,128]{2,1,0:T(8,128)S(1)} fusion(bf16[384,128,128]{2,1,0:T(8,128)(2,1)} %get-tuple-element.428, s32[]{:T(128)S(6)} %select_n.125, f32[64,16,128]{2,1,0:T(8,128)S(1)} %gather_fusion, pred[64]{0:T(512)(128)(4,1)S(1)} %get-tuple-element.390, pred[64]{0:T(512)(128)(4,1)S(1)} %dynamic_slice.78), kind=kOutput, calls=%fused_computation.6.clone.1 | convolution fusion | flops 201588736 | bytes 3145860 | tf_op jit(solution)/shard_map/while/body/eval_jaxpr/tij,mtj->mti/dot_general | solution.py:40
  130.4 5.0 %fusion.50 = f32[64,16,128]{2,1,0:T(8,128)S(1)} fusion(bf16[384,128,128]{2,1,0:T(8,128)(2,1)} %get-tuple-element.428, s32[]{:T(128)S(6)} %select_n.125, f32[64,16,128]{2,1,0:T(8,128)S(1)} %gather_fusion, pred[64]{0:T(512)(128)(4,1)S(1)} %get-tuple-element.390, pred[64]{0:T(512)(128)(4,1)S(1)} %dynamic_slice.78), kind=kOutput, calls=%fused_computation.6.clone.1 | convolution fusion | flops 201588736 | bytes 3145860 | tf_op jit(solution)/shard_map/while/body/eval_jaxpr/tij,mtj->mti/dot_general | solution.py:40
  135.5 2.9 scatter_fusion
  139.2 5.0 %fusion.50 = f32[64,16,128]{2,1,0:T(8,128)S(1)} fusion(bf16[384,128,128]{2,1,0:T(8,128)(2,1)} %get-tuple-element.428, s32[]{:T(128)S(6)} %select_n.125, f32[64,16,128]{2,1,0:T(8,128)S(1)} %gather_fusion, pred[64]{0:T(512)(128)(4,1)S(1)} %get-tuple-element.390, pred[64]{0:T(512)(128)(4,1)S(1)} %dynamic_slice.78), kind=kOutput, calls=%fused_computation.6.clone.1 | convolution fusion | flops 201588736 | bytes 3145860 | tf_op jit(solution)/shard_map/while/body/eval_jaxpr/tij,mtj->mti/dot_general | solution.py:40
  144.2 2.9 scatter_fusion
  147.9 5.0 %fusion.50 = f32[64,16,128]{2,1,0:T(8,128)S(1)} fusion(bf16[384,128,128]{2,1,0:T(8,128)(2,1)} %get-tuple-element.428, s32[]{:T(128)S(6)} %select_n.125, f32[64,16,128]{2,1,0:T(8,128)S(1)} %gather_fusion, pred[64]{0:T(512)(128)(4,1)S(1)} %get-tuple-element.390, pred[64]{0:T(512)(128)(4,1)S(1)} %dynamic_slice.78), kind=kOutput, calls=%fused_computation.6.clone.1 | convolution fusion | flops 201588736 | bytes 3145860 | tf_op jit(solution)/shard_map/while/body/eval_jaxpr/tij,mtj->mti/dot_general | solution.py:40
  153.0 2.9 scatter_fusion
  156.7 5.0 %fusion.50 = f32[64,16,128]{2,1,0:T(8,128)S(1)} fusion(bf16[384,128,128]{2,1,0:T(8,128)(2,1)} %get-tuple-element.428, s32[]{:T(128)S(6)} %select_n.125, f32[64,16,128]{2,1,0:T(8,128)S(1)} %gather_fusion, pred[64]{0:T(512)(128)(4,1)S(1)} %get-tuple-element.390, pred[64]{0:T(512)(128)(4,1)S(1)} %dynamic_slice.78), kind=kOutput, calls=%fused_computation.6.clone.1 | convolution fusion | flops 201588736 | bytes 3145860 | tf_op jit(solution)/shard_map/while/body/eval_jaxpr/tij,mtj->mti/dot_general | solution.py:40
  161.8 2.9 scatter_fusion
  167.2 43.1 %while.27 = (s32[]{:T(128)}, f32[16,64,128]{2,0,1:T(8,128)S(1)}, s32[384]{0:T(512)S(1)}, pred[384]{0:T(512)(128)(4,1)S(1)}, s32[384]{0:T(512)S(1)}, /*index=5*/f...) while((s32[]{:T(128)}, f32[16,64,128]{2,0,1:T(8,128)S(1)}, ...), condition=%wide.region_13.15_spmd, body=%wide.region_11.14_spmd.sunk | while | flops 201721408 | bytes 5773547 | solution.py:59
  168.0 3.4 fusion.53
  171.5 2.9 scatter_fusion.1
  175.2 3.4 fusion.53
  178.7 2.9 scatter_fusion.1
  182.4 3.4 fusion.53
  185.9 2.9 scatter_fusion.1
  189.6 3.4 fusion.53
  193.1 2.9 scatter_fusion.1
  196.8 3.4 fusion.53
  200.2 2.9 scatter_fusion.1
  204.0 3.4 fusion.53
  207.4 2.9 scatter_fusion.1
  211.5 14.1 %reduce-scatter.3.cloned.1.call-done = f32[16,1024]{1,0:T(8,128)} async-done(((f32[16,16384]{1,0:T(8,128)}), f32[16,1024]{1,0:T(8,128)}) %reduce-scatter.3.cloned.1.call-update) | async-done | bytes 65552 | tf_op jit(solution)/shard_map/reduce_scatter | solution.py:60
  225.6 74.7 %reduce-scatter.5.cloned.1.call-done = f32[16,1024]{1,0:T(8,128)} async-done(((f32[16,8192]{1,0:T(8,128)}), f32[16,1024]{1,0:T(8,128)}) %reduce-scatter.5.cloned.1.call-update) | async-done | bytes 65552 | tf_op jit(solution)/shard_map/reduce_scatter | solution.py:63
  301.5 66.6 %all-reduce = (f32[48,48]{0,1:T(8,128)S(1)}, f32[48,48]{1,0:T(8,128)S(1)}) all-reduce(f32[48,48]{0,1:T(8,128)S(1)} %fusion.23, f32[48,48]{1,0:T(8,128)S(1)} %fusion.22), channel_id=1, replica_groups=mesh['row'=8,'col'=16] {'row','col'}, use_global_device_ids=true, to_apply=%region_4.5 | all-reduce | flops 4608 | bytes 36864 | tf_op jit(solution)/shard_map/psum | solution.py:81
  368.1 4.4 %cholesky.18 = f32[48,48]{1,0:T(8,128)S(1)} custom-call(f32[48,48]{1,0:T(8,128)S(1)} %fusion.31), custom_call_target="Cholesky" | custom-call | tf_op jit(solution)/shard_map/jit(cholesky)/cholesky | solution.py:85
  373.8 3.7 custom-call.13
  (102 shorter events, 26.9 us)
Async XLA Ops:
  7.2 158.6 %all-gather.2.cloned.1.call-start = ((), (), s32[]{:S(2)}) async-start(), calls=%async_computation.3 | async-start | bytes 1114112 | tf_op jit(solution)/shard_map/all_gather | solution.py:23
  78.5 147.1 %reduce-scatter.3.cloned.1.call-start = ((), (), s32[]{:S(2)}) async-start(), calls=%async_computation.2 | async-start | bytes 1114112 | tf_op jit(solution)/shard_map/reduce_scatter | solution.py:60
  165.7 134.5 %reduce-scatter.5.cloned.1.call-start = ((), (), s32[]{:S(2)}) async-start(), calls=%async_computation.4 | async-start | bytes 589824 | tf_op jit(solution)/shard_map/reduce_scatter | solution.py:63
  167.1 44.0 %copy-start = (f32[16,1024]{1,0:T(8,128)S(1)}, f32[16,1024]{1,0:T(8,128)}, u32[]{:S(2)}) copy-start(f32[16,1024]{1,0:T(8,128)} %multiply_subtract_fusion) | copy-start | bytes 196612
  167.2 44.0 %copy-start.2 = (f32[16,1024]{1,0:T(8,128)S(1)}, f32[16,1024]{1,0:T(8,128)}, u32[]{:S(2)}) copy-start(f32[16,1024]{1,0:T(8,128)} %param.18) | copy-start | bytes 196612
  167.2 44.0 %copy-start.4 = (f32[16,1024]{1,0:T(8,128)S(1)}, f32[16,1024]{1,0:T(8,128)}, u32[]{:S(2)}) copy-start(f32[16,1024]{1,0:T(8,128)} %param.20) | copy-start | bytes 196612
  167.2 134.0 %copy-start.1 = (f32[16,1024]{1,0:T(8,128)S(1)}, f32[16,1024]{1,0:T(8,128)}, u32[]{:S(2)}) copy-start(f32[16,1024]{1,0:T(8,128)} %param.19) | copy-start | bytes 196612
  167.2 134.0 %copy-start.3 = (f32[16,1024]{1,0:T(8,128)S(1)}, f32[16,1024]{1,0:T(8,128)}, u32[]{:S(2)}) copy-start(f32[16,1024]{1,0:T(8,128)} %param.21) | copy-start | bytes 196612
Sparse Core Ops, SparseCore 0:
  78.6 29.4 all-gather.1
  165.8 59.7 reduce-scatter.2
  229.5 70.6 reduce-scatter.4
where the time goes:
time: 388 us; the launch traced here: 387 us
  blocking collectives  167 us (43%)
  waiting for transfers between devices  88.8 us (23%)
  matrix products  53.9 us (14%)
  other arithmetic  50.7 us (13%)
  between operations  14.6 us (4%)
  local copies, waits for them, and re-layouts  12 us (3%)
    reduce_scatter x1, waiting for transfers between devices, hamiltonian(): lax.psum_scatter(col_totals.reshape(members, -1), 'row', scatter_dimensio...  74.7 us
    psum x1, blocking collectives, on_device(): lax.psum((jnp.sum(vectors * hvectors, axis=1), jnp.sum(vectors * vectors,...  68.7 us
    psum x1, blocking collectives, on_device(): lax.psum((dense_product(basis_rows, basis_rows.T), dense_product(basis_ro...  66.6 us
    all_gather x1, blocking collectives, hamiltonian(): col_range = lax.all_gather(operand, 'row', axis=1, tiled=True)  31.3 us
    dot_general x6, matrix products, forward_product(): jnp.einsum('tij,mtj->mti', tile_part, inputs, precision=HIGHEST_PRECISION)  29.9 us
    dot_general x6, matrix products, backward_product(): jnp.einsum('tij,mti->mtj', tile_part, inputs, precision=HIGHEST_PRECISION)  20.4 us
    scatter-add x6, other arithmetic, backward(): return totals.at[:, col_part, :].add(jnp.where(live_part, product, 0.0))  17.2 us
    scatter-add x6, other arithmetic, forward(): return totals.at[:, row_part, :].add(jnp.where(live_part, product, 0.0))  17.2 us
  transfers between devices with their start and end apart: 3, of which 2 were waited for; matrix products, arithmetic and copies ran while one was open for 26% of the time, Pallas kernels for 0%

commit v1 on v0

--- a/solution.py
+++ b/solution.py
@@ -71,7 +71,8 @@
 ):
     total_rows = vectors.shape[1] * lax.axis_size("row") * lax.axis_size("col")
     rayleigh_top, rayleigh_bottom = lax.psum(
-        (jnp.sum(vectors * hvectors, axis=1), jnp.sum(vectors * vectors, axis=1)), ("row", "col")
+        lax.psum((jnp.sum(vectors * hvectors, axis=1), jnp.sum(vectors * vectors, axis=1)), "row"),
+        "col",
     )
     ritz_values = rayleigh_top / (rayleigh_bottom + EPSILON)
     residual = hvectors - ritz_values[:, None] * vectors

time: 388 us -> 371 us (0.956)
  blocking collectives: 167 us -> 150 us
    psum x1, blocking collectives: 68.7 us -> 22.6 us  [on_device(): lax.psum((jnp.sum(vectors * hvectors, axis=1), jnp.sum(vectors * vectors,...]
    psum x0 -> x1, blocking collectives: none -> 30.9 us  [on_device(): lax.psum(lax.psum((jnp.sum(vectors * hvectors, axis=1), jnp.sum(vectors *...]
  transfers between devices with their start and end apart: 3 -> 3, of which waited for: 2 -> 2; matrix products, arithmetic and copies ran while one was open for 26% -> 27% of each run, Pallas kernels for 0% -> 0%
where the time goes in v1:
time: 371 us; the launch traced here: 370 us
  blocking collectives  150 us (40%)
  waiting for transfers between devices  87.9 us (24%)
  matrix products  53.9 us (15%)
  other arithmetic  50.7 us (14%)
  between operations  14.6 us (4%)
  local copies, waits for them, and re-layouts  12 us (3%)
    reduce_scatter x1, waiting for transfers between devices, hamiltonian(): lax.psum_scatter(col_totals.reshape(members, -1), 'row', scatter_dimensio...  75 us
    psum x1, blocking collectives, on_device(): lax.psum((dense_product(basis_rows, basis_rows.T), dense_product(basis_ro...  66.6 us
    psum x1, blocking collectives, on_device(): lax.psum(lax.psum((jnp.sum(vectors * hvectors, axis=1), jnp.sum(vectors *...  30.9 us
    all_gather x1, blocking collectives, hamiltonian(): col_range = lax.all_gather(operand, 'row', axis=1, tiled=True)  30 us
    dot_general x6, matrix products, forward_product(): jnp.einsum('tij,mtj->mti', tile_part, inputs, precision=HIGHEST_PRECISION)  29.9 us
    psum x1, blocking collectives, on_device(): lax.psum((jnp.sum(vectors * hvectors, axis=1), jnp.sum(vectors * vectors,...  22.6 us
    dot_general x6, matrix products, backward_product(): jnp.einsum('tij,mti->mtj', tile_part, inputs, precision=HIGHEST_PRECISION)  20.4 us
    scatter-add x6, other arithmetic, backward(): return totals.at[:, col_part, :].add(jnp.where(live_part, product, 0.0))  17.2 us
  transfers between devices with their start and end apart: 3, of which 2 were waited for; matrix products, arithmetic and copies ran while one was open for 27% of the time, Pallas kernels for 0%

profile of v1, /device:TPU:1, one launch (start us, length us, event | category | flops | bytes accessed | tf_op | source)
XLA Modules:
  0.0 369.8 jit_solution(15260614360546134591)
XLA Ops:
  8.2 22.6 %all-reduce.2 = (f32[16]{0:T(128)S(1)}, f32[16]{0:T(128)S(1)}) all-reduce(f32[16]{0:T(128)S(1)} %get-tuple-element.269, f32[16]{0:T(128)S(1)} %get-tuple-element.268), channel_id=1, replica_groups=mesh['row'=8,'col'=16] {'row'}, use_global_device_ids=true, to_apply=%region_1.0 | all-reduce | flops 32 | bytes 256 | tf_op jit(solution)/shard_map/psum | solution.py:74
  30.8 30.9 %all-reduce.1 = (f32[16]{0:T(128)S(1)}, f32[16]{0:T(128)S(1)}) all-reduce(f32[16]{0:T(128)S(1)} %get-tuple-element.302, f32[16]{0:T(128)S(1)} %get-tuple-element.303), channel_id=1, replica_groups=mesh['row'=8,'col'=16] {'col'}, use_global_device_ids=true, to_apply=%region_2.0 | all-reduce | flops 32 | bytes 256 | tf_op jit(solution)/shard_map/psum | solution.py:73
  63.4 30.0 %all_gather.6 = f32[16,8192]{1,0:T(8,128)S(1)} all-gather(f32[16,1024]{1,0:T(8,128)} %multiply_subtract_fusion), channel_id=1, replica_groups=mesh['row'=8,'col'=16] {'row'}, dimensions={1}, use_global_device_ids=true | all-gather | bytes 589824 | tf_op jit(solution)/shard_map/all_gather | solution.py:24
  95.6 52.6 %while.26 = (s32[]{:T(128)}, f32[16,128,128]{2,0,1:T(8,128)S(1)}, s32[384]{0:T(512)S(1)}, pred[384]{0:T(512)(128)(4,1)S(1)}, s32[384]{0:T(512)S(1)}, /*index=5*/...) while((s32[]{:T(128)}, f32[16,128,128]{2,0,1:T(8,128)S(1)}, ...), condition=%wide.region_11.13_spmd, body=%wide.region_9.12_spmd.sunk | while | flops 201721408 | bytes 5773547 | solution.py:58
  96.4 5.0 %fusion.50 = f32[64,16,128]{2,1,0:T(8,128)S(1)} fusion(bf16[384,128,128]{2,1,0:T(8,128)(2,1)} %get-tuple-element.430, s32[]{:T(128)S(6)} %select_n.125, f32[64,16,128]{2,1,0:T(8,128)S(1)} %gather_fusion, pred[64]{0:T(512)(128)(4,1)S(1)} %get-tuple-element.392, pred[64]{0:T(512)(128)(4,1)S(1)} %dynamic_slice.78), kind=kOutput, calls=%fused_computation.6.clone.1 | convolution fusion | flops 201588736 | bytes 3145860 | tf_op jit(solution)/shard_map/while/body/eval_jaxpr/tij,mtj->mti/dot_general | solution.py:40
  105.2 5.0 %fusion.50 = f32[64,16,128]{2,1,0:T(8,128)S(1)} fusion(bf16[384,128,128]{2,1,0:T(8,128)(2,1)} %get-tuple-element.430, s32[]{:T(128)S(6)} %select_n.125, f32[64,16,128]{2,1,0:T(8,128)S(1)} %gather_fusion, pred[64]{0:T(512)(128)(4,1)S(1)} %get-tuple-element.392, pred[64]{0:T(512)(128)(4,1)S(1)} %dynamic_slice.78), kind=kOutput, calls=%fused_computation.6.clone.1 | convolution fusion | flops 201588736 | bytes 3145860 | tf_op jit(solution)/shard_map/while/body/eval_jaxpr/tij,mtj->mti/dot_general | solution.py:40
  113.9 5.0 %fusion.50 = f32[64,16,128]{2,1,0:T(8,128)S(1)} fusion(bf16[384,128,128]{2,1,0:T(8,128)(2,1)} %get-tuple-element.430, s32[]{:T(128)S(6)} %select_n.125, f32[64,16,128]{2,1,0:T(8,128)S(1)} %gather_fusion, pred[64]{0:T(512)(128)(4,1)S(1)} %get-tuple-element.392, pred[64]{0:T(512)(128)(4,1)S(1)} %dynamic_slice.78), kind=kOutput, calls=%fused_computation.6.clone.1 | convolution fusion | flops 201588736 | bytes 3145860 | tf_op jit(solution)/shard_map/while/body/eval_jaxpr/tij,mtj->mti/dot_general | solution.py:40
  119.0 2.9 scatter_fusion
  122.7 5.0 %fusion.50 = f32[64,16,128]{2,1,0:T(8,128)S(1)} fusion(bf16[384,128,128]{2,1,0:T(8,128)(2,1)} %get-tuple-element.430, s32[]{:T(128)S(6)} %select_n.125, f32[64,16,128]{2,1,0:T(8,128)S(1)} %gather_fusion, pred[64]{0:T(512)(128)(4,1)S(1)} %get-tuple-element.392, pred[64]{0:T(512)(128)(4,1)S(1)} %dynamic_slice.78), kind=kOutput, calls=%fused_computation.6.clone.1 | convolution fusion | flops 201588736 | bytes 3145860 | tf_op jit(solution)/shard_map/while/body/eval_jaxpr/tij,mtj->mti/dot_general | solution.py:40
  127.8 2.9 scatter_fusion
  131.5 5.0 %fusion.50 = f32[64,16,128]{2,1,0:T(8,128)S(1)} fusion(bf16[384,128,128]{2,1,0:T(8,128)(2,1)} %get-tuple-element.430, s32[]{:T(128)S(6)} %select_n.125, f32[64,16,128]{2,1,0:T(8,128)S(1)} %gather_fusion, pred[64]{0:T(512)(128)(4,1)S(1)} %get-tuple-element.392, pred[64]{0:T(512)(128)(4,1)S(1)} %dynamic_slice.78), kind=kOutput, calls=%fused_computation.6.clone.1 | convolution fusion | flops 201588736 | bytes 3145860 | tf_op jit(solution)/shard_map/while/body/eval_jaxpr/tij,mtj->mti/dot_general | solution.py:40
  136.5 2.9 scatter_fusion
  140.3 5.0 %fusion.50 = f32[64,16,128]{2,1,0:T(8,128)S(1)} fusion(bf16[384,128,128]{2,1,0:T(8,128)(2,1)} %get-tuple-element.430, s32[]{:T(128)S(6)} %select_n.125, f32[64,16,128]{2,1,0:T(8,128)S(1)} %gather_fusion, pred[64]{0:T(512)(128)(4,1)S(1)} %get-tuple-element.392, pred[64]{0:T(512)(128)(4,1)S(1)} %dynamic_slice.78), kind=kOutput, calls=%fused_computation.6.clone.1 | convolution fusion | flops 201588736 | bytes 3145860 | tf_op jit(solution)/shard_map/while/body/eval_jaxpr/tij,mtj->mti/dot_general | solution.py:40
  145.3 2.9 scatter_fusion
  150.8 43.1 %while.27 = (s32[]{:T(128)}, f32[16,64,128]{2,0,1:T(8,128)S(1)}, s32[384]{0:T(512)S(1)}, pred[384]{0:T(512)(128)(4,1)S(1)}, s32[384]{0:T(512)S(1)}, /*index=5*/f...) while((s32[]{:T(128)}, f32[16,64,128]{2,0,1:T(8,128)S(1)}, ...), condition=%wide.region_15.17_spmd, body=%wide.region_13.16_spmd.sunk | while | flops 201721408 | bytes 5773547 | solution.py:59
  151.6 3.4 fusion.53
  155.1 2.9 scatter_fusion.1
  158.8 3.4 fusion.53
  162.2 2.9 scatter_fusion.1
  165.9 3.4 fusion.53
  169.4 2.9 scatter_fusion.1
  173.1 3.4 fusion.53
  176.6 2.9 scatter_fusion.1
  180.3 3.4 fusion.53
  183.8 2.9 scatter_fusion.1
  187.5 3.4 fusion.53
  191.0 2.9 scatter_fusion.1
  195.1 12.8 %reduce-scatter.3.cloned.1.call-done = f32[16,1024]{1,0:T(8,128)} async-done(((f32[16,16384]{1,0:T(8,128)}), f32[16,1024]{1,0:T(8,128)}) %reduce-scatter.3.cloned.1.call-update) | async-done | bytes 65552 | tf_op jit(solution)/shard_map/reduce_scatter | solution.py:60
  207.9 75.0 %reduce-scatter.5.cloned.1.call-done = f32[16,1024]{1,0:T(8,128)} async-done(((f32[16,8192]{1,0:T(8,128)}), f32[16,1024]{1,0:T(8,128)}) %reduce-scatter.5.cloned.1.call-update) | async-done | bytes 65552 | tf_op jit(solution)/shard_map/reduce_scatter | solution.py:63
  284.1 66.6 %all-reduce = (f32[48,48]{0,1:T(8,128)S(1)}, f32[48,48]{1,0:T(8,128)S(1)}) all-reduce(f32[48,48]{0,1:T(8,128)S(1)} %fusion.23, f32[48,48]{1,0:T(8,128)S(1)} %fusion.22), channel_id=1, replica_groups=mesh['row'=8,'col'=16] {'row','col'}, use_global_device_ids=true, to_apply=%region_6.7 | all-reduce | flops 4608 | bytes 36864 | tf_op jit(solution)/shard_map/psum | solution.py:82
  350.8 4.4 %cholesky.18 = f32[48,48]{1,0:T(8,128)S(1)} custom-call(f32[48,48]{1,0:T(8,128)S(1)} %fusion.31), custom_call_target="Cholesky" | custom-call | tf_op jit(solution)/shard_map/jit(cholesky)/cholesky | solution.py:86
  356.5 3.7 custom-call.13
  (103 shorter events, 29.8 us)
Async XLA Ops:
  7.2 142.2 %all-gather.2.cloned.1.call-start = ((), (), s32[]{:S(2)}) async-start(), calls=%async_computation.3 | async-start | bytes 1114112 | tf_op jit(solution)/shard_map/all_gather | solution.py:23
  63.3 144.5 %reduce-scatter.3.cloned.1.call-start = ((), (), s32[]{:S(2)}) async-start(), calls=%async_computation.2 | async-start | bytes 1114112 | tf_op jit(solution)/shard_map/reduce_scatter | solution.py:60
  149.3 133.6 %reduce-scatter.5.cloned.1.call-start = ((), (), s32[]{:S(2)}) async-start(), calls=%async_computation.4 | async-start | bytes 589824 | tf_op jit(solution)/shard_map/reduce_scatter | solution.py:63
  150.7 44.0 %copy-start = (f32[16,1024]{1,0:T(8,128)S(1)}, f32[16,1024]{1,0:T(8,128)}, u32[]{:S(2)}) copy-start(f32[16,1024]{1,0:T(8,128)} %multiply_subtract_fusion) | copy-start | bytes 196612
  150.7 44.0 %copy-start.2 = (f32[16,1024]{1,0:T(8,128)S(1)}, f32[16,1024]{1,0:T(8,128)}, u32[]{:S(2)}) copy-start(f32[16,1024]{1,0:T(8,128)} %param.18) | copy-start | bytes 196612
  150.7 44.0 %copy-start.4 = (f32[16,1024]{1,0:T(8,128)S(1)}, f32[16,1024]{1,0:T(8,128)}, u32[]{:S(2)}) copy-start(f32[16,1024]{1,0:T(8,128)} %param.20) | copy-start | bytes 196612
  150.7 133.0 %copy-start.1 = (f32[16,1024]{1,0:T(8,128)S(1)}, f32[16,1024]{1,0:T(8,128)}, u32[]{:S(2)}) copy-start(f32[16,1024]{1,0:T(8,128)} %param.19) | copy-start | bytes 196612
  150.8 133.0 %copy-start.3 = (f32[16,1024]{1,0:T(8,128)S(1)}, f32[16,1024]{1,0:T(8,128)}, u32[]{:S(2)}) copy-start(f32[16,1024]{1,0:T(8,128)} %param.21) | copy-start | bytes 196612
Sparse Core Ops, SparseCore 0:
  63.5 27.3 all-gather.1
  149.4 58.4 reduce-scatter.2
  211.8 71.0 reduce-scatter.4
